TPU v7x, 32 devices: a whole 2x2x4 slice. The times are simulated.
32 devices in a mesh: dp: 2 (over core), expert: 16 (over z, y, x).
Axes of the slice: x: 2, y: 2, z: 4, core: 2. Of those that a mesh axis runs over, the one named last changes fastest.
Arguments:
- tokens: bfloat16 [4096, 1152], P(('dp', 'expert')), may hold values from -6 to 6
- out_grad: bfloat16 [4096, 1152], P(('dp', 'expert')), may hold values from -6 to 6
- gates: float32 [4096, 2], P(('dp', 'expert')), may hold values from 0.05 to 1
- expert_ids: int32 [4096, 2], P(('dp', 'expert')), may hold values from 0 to 15, all different within a row; in each aligned block of 128 rows (0 to 127, 128 to 255, ...) at most 24 rows name the same one
- swap_list: int32 [16], replicated, may hold values from 0 to 15, as said below
- w_in: bfloat16 [16, 1152, 3072], P('expert', None, 'dp'), may hold values from -0.1875 to 0.1875
- w_out: bfloat16 [16, 3072, 1152], P('expert', 'dp'), may hold values from -0.109375 to 0.109375
- first_moment: float32 [16, 1152, 3072], P('expert', None, 'dp'), may hold values from -12 to 12
- second_moment: float32 [16, 1152, 3072], P('expert', None, 'dp'), may hold values from 1 to 100
Outputs:
- x_grad: bfloat16 [4096, 1152], P(('dp', 'expert'))
- adam_out: bfloat16 [16, 1152, 3072], P('expert', None, 'dp')
Inputs may be any that keep to these rules, and one draw needn't show every extreme that they name: `expert_ids`: among the 128 tokens of one device no expert is named by more than 24 rows; a token's two experts differ. swap_list[e] is e or e XOR 16/2, and swap_list[swap_list[e]] = e; swap_list[0] = 8 and swap_list[15] = 7.
All inputs are finite; a program needn't handle non-finite values.
Results may differ from a plain program's by a relative error of at most 0.015.
Values may be sent and summed in bfloat16 or wider, within the bound.
No kernel may reach another device: no remote copies, remote signals or barrier semaphores. Data moves between devices by JAX's collectives and lax.ppermute only.
A program may use at most 128 MiB of HBM per device.

v0:
```python
import jax
import jax.numpy as jnp
from jax import lax
from jax.sharding import PartitionSpec as P

ADAM_STEP = 100
coef_c = 0.7978845608028654
coef_a = 0.044715
beta_one = 0.9
beta_two = 0.999
adam_eps = 1e-08


def partner(block, axis, apart):
    count = lax.axis_size(axis)
    route = []
    for low in range(count):
        high = low | 1 << apart
        if high != low and high < count:
            route += [(low, high), (high, low)]
    return lax.ppermute(block, axis, route)


def gelu_slope(pre_act):
    inner_arg = coef_c * (pre_act + coef_a * pre_act * pre_act * pre_act)
    tanh_val = jnp.tanh(inner_arg)
    return 0.5 * (1.0 + tanh_val) + 0.5 * pre_act * (1.0 - tanh_val * tanh_val) * coef_c * (
        1.0 + 3.0 * coef_a * pre_act * pre_act
    )


def pack_rows(id_block, x_block, g_block, dest_table, capacity):
    expert_count = dest_table.shape[0]
    flat_ids = id_block.reshape(-1)
    assigned = flat_ids.shape[0]
    lane_ids = jnp.arange(expert_count, dtype=jnp.int32)
    id_onehot = (flat_ids[:, None] == lane_ids[None, :]).astype(jnp.int32)
    dest_dev = jnp.sum(id_onehot * dest_table[None, :], axis=1)
    onehot = (dest_dev[:, None] == lane_ids[None, :]).astype(jnp.int32)
    before = jnp.cumsum(onehot, axis=0) - onehot
    slot_idx = jnp.sum(before * onehot, axis=1)
    where_to = dest_dev * capacity + slot_idx
    source = (
        jnp.zeros((expert_count * capacity,), jnp.int32)
        .at[where_to]
        .set(jnp.arange(assigned, dtype=jnp.int32) + 1)
    )
    filled = (source > 0)[:, None]
    pick_idx = jnp.maximum(source - 1, 0)
    model_width = x_block.shape[1]
    x_rows = jnp.where(
        filled, jnp.take(x_block, pick_idx // 2, axis=0), jnp.zeros((), jnp.bfloat16)
    )
    g_rows = jnp.where(
        filled,
        jnp.take(g_block.reshape(assigned, model_width), pick_idx, axis=0),
        jnp.zeros((), jnp.bfloat16),
    )
    return (
        x_rows.reshape(expert_count, capacity, model_width),
        g_rows.reshape(expert_count, capacity, model_width),
        where_to,
    )


def shards(
    tokens, out_grad, gates, expert_ids, swap_list, w_in, w_out, first_moment, second_moment
):
    expert_count = lax.axis_size("expert")
    top_bit = expert_count.bit_length() - 2
    own_index = lax.axis_index("expert")
    lane_ids = jnp.arange(expert_count, dtype=jnp.int32)
    partner_me = jnp.sum(jnp.where(lane_ids == own_index, swap_list, 0))
    is_moved = partner_me != own_index
    tok_count = tokens.shape[0]
    model_width = tokens.shape[1]
    capacity = 3 * tok_count // expert_count
    grad_pair = (gates[:, :, None] * out_grad[:, None, :].astype(jnp.float32)).astype(jnp.bfloat16)
    x_buf, g_buf, where_to = pack_rows(expert_ids, tokens, grad_pair, lane_ids, capacity)
    x_recv, g_recv = (
        lax.all_to_all(x_buf, "expert", split_axis=0, concat_axis=0, tiled=True),
        lax.all_to_all(g_buf, "expert", split_axis=0, concat_axis=0, tiled=True),
    )
    x_all, g_all = (
        lax.all_gather(x_recv, "dp", axis=0, tiled=True),
        lax.all_gather(g_recv, "dp", axis=0, tiled=True),
    )
    x_rows = x_all.reshape(-1, model_width)
    g_rows = g_all.reshape(-1, model_width)
    w_in_local = w_in[0]
    w_out_local = w_out[0]
    pre_act = jnp.dot(x_rows, w_in_local, preferred_element_type=jnp.float32)
    act_grad = lax.dot_general(
        g_rows, w_out_local, (((1,), (1,)), ((), ())), preferred_element_type=jnp.float32
    )
    pre_grad = (act_grad * gelu_slope(pre_act)).astype(jnp.bfloat16)
    own_rows = lax.psum_scatter(
        lax.dot_general(
            pre_grad, w_in_local, (((1,), (1,)), ((), ())), preferred_element_type=jnp.float32
        ).astype(jnp.bfloat16),
        "dp",
        scatter_dimension=0,
        tiled=True,
    )
    returned = lax.all_to_all(
        own_rows.reshape(expert_count, capacity, model_width),
        "expert",
        split_axis=0,
        concat_axis=0,
        tiled=True,
    )
    picked = jnp.take(
        returned.reshape(expert_count * capacity, model_width), where_to, axis=0
    ).astype(jnp.float32)
    x_grad = jnp.sum(picked.reshape(tok_count, 2, model_width), axis=1).astype(jnp.bfloat16)
    weight_grad = lax.dot_general(
        x_rows, pre_grad, (((0,), (0,)), ((), ())), preferred_element_type=jnp.float32
    )
    first_new = beta_one * first_moment[0] + (1.0 - beta_one) * weight_grad
    second_new = beta_two * second_moment[0] + (1.0 - beta_two) * weight_grad * weight_grad
    adam_out = (
        first_new
        / (1.0 - beta_one**ADAM_STEP)
        / (jnp.sqrt(second_new / (1.0 - beta_two**ADAM_STEP)) + adam_eps)
    )
    adam_out = adam_out.astype(jnp.bfloat16)[None]
    swapped_step = partner(adam_out, "expert", top_bit)
    adam_out = jnp.where(is_moved, swapped_step, adam_out)
    return (x_grad, adam_out)


def solution(mesh):
    in_specs = (
        P(("dp", "expert"), None),
        P(("dp", "expert"), None),
        P(("dp", "expert"), None),
        P(("dp", "expert"), None),
        P(),
        P("expert", None, "dp"),
        P("expert", "dp", None),
        P("expert", None, "dp"),
        P("expert", None, "dp"),
    )
    out_specs = (P(("dp", "expert"), None), P("expert", None, "dp"))
    return jax.shard_map(shards, mesh=mesh, in_specs=in_specs, out_specs=out_specs, check_vma=False)
```

profile of v0, /device:TPU:17, one launch (start us, length us, event | category | flops | bytes accessed | tf_op | source)
XLA Modules:
  0.0 331.9 jit_solution(17654201795168940946)
XLA Ops:
  7.8 1.7 copy.14
  9.6 1.0 eq.46
  11.7 1.3 reduce-window.6
  13.8 1.3 reduce-window.9
  17.1 1.6 scatter_custom_fusion
  20.6 1.4 broadcast_in_dim.72
  22.0 1.3 broadcast_in_dim.77
  24.0 2.3 mul.129
  26.2 3.0 mul.130
  29.2 1.4 copy.16
  30.6 1.5 mul.127
  32.2 4.6 %gather_fusion.1 = bf16[384,1152]{1,0:T(8,128)(2,1)} fusion(bf16[128,1152]{1,0:T(8,128)(2,1)} %param.9, s32[1024]{0:T(1024)S(1)} %pad_clamp_fusion.1), kind=kCustom, calls=%fused_computation.1 | custom fusion | bytes 1771008 | tf_op jit(solution)/shard_map/jit(_take)/gather | solution.py:52
  36.8 2.2 multiply_convert_fusion
  39.0 4.7 %gather_fusion = bf16[384,1152]{1,0:T(8,128)(2,1)} fusion(bf16[256,1152]{1,0:T(8,128)(2,1)} %multiply_convert_fusion, s32[1024]{0:T(1024)S(1)} %pad_clamp_fusion.2), kind=kCustom, calls=%fused_computation | custom fusion | bytes 1771008 | tf_op jit(solution)/shard_map/jit(_take)/gather | solution.py:56
  43.8 2.7 select_select_fusion.1
  46.5 27.4 %all_to_all.15 = bf16[16,24,1152]{2,1,0:T(8,128)(2,1)} all-to-all(bf16[16,24,1152]{2,1,0:T(8,128)(2,1)S(1)} %get-tuple-element.5), channel_id=1, replica_groups=mesh['dp'=2,'expert'=16] {'expert'}, dimensions={0} | all-to-all | bytes 1769472 | tf_op jit(solution)/shard_map/all_to_all | solution.py:81
  74.0 25.3 %all_to_all.16 = bf16[16,24,1152]{2,1,0:T(8,128)(2,1)} all-to-all(bf16[16,24,1152]{2,1,0:T(8,128)(2,1)} %get-tuple-element.4), channel_id=1, replica_groups=mesh['dp'=2,'expert'=16] {'expert'}, dimensions={0} | all-to-all | bytes 1769472 | tf_op jit(solution)/shard_map/all_to_all | solution.py:82
  99.6 6.4 %fusion.16 = f32[768,1536]{1,0:T(8,128)} fusion(bf16[768,1152]{1,0:T(8,128)(2,1)} %bitcast.68, bf16[1,1152,1536]{2,1,0:T(8,128)(2,1)S(1)} %copy-done), kind=kOutput, calls=%fused_computation.24 | convolution fusion | flops 2717908992 | bytes 10027008 | tf_op jit(solution)/shard_map/dot_general | solution.py:92
  106.0 5.5 %all-gather.3.cloned.1.call-done = bf16[32,24,1152]{2,1,0:T(8,128)(2,1)} async-done(((bf16[16,24,1152]{2,1,0:T(8,128)(2,1)}), bf16[32,24,1152]{2,1,0:T(8,128)(2,1)}) %all-gather.3.cloned.1.call-update) | async-done | bytes 1769488 | tf_op jit(solution)/shard_map/all_gather | solution.py:86
  111.4 8.0 %fusion.13 = bf16[768,1536]{1,0:T(8,128)(2,1)S(1)} fusion(f32[768,1536]{1,0:T(8,128)} %fusion.16, bf16[768,1152]{1,0:T(8,128)(2,1)} %bitcast.70, bf16[1,1536,1152]{2,1,0:T(8,128)(2,1)} %param.15), kind=kOutput, calls=%fused_computation.21 | convolution fusion | flops 2740322304 | bytes 12386304 | tf_op jit(solution)/shard_map/dot_general | solution.py:93
  119.4 1.4 copy-done.4
  120.8 4.4 %fusion.20 = bf16[768,1152]{1,0:T(8,128)(2,1)} fusion(bf16[768,1536]{1,0:T(8,128)(2,1)S(1)} %fusion.13, bf16[1,1152,1536]{2,1,0:T(8,128)(2,1)S(1)} %copy-done), kind=kOutput, calls=%fused_computation.29 | convolution fusion | flops 2718793728 | bytes 7667712 | tf_op jit(solution)/shard_map/dot_general | solution.py:98
  125.2 15.1 %fusion.19 = bf16[1,1152,1536]{2,1,0:T(8,128)(2,1)} fusion(f32[1,1152,1536]{2,1,0:T(8,128)} %param.17, f32[1,1152,1536]{2,1,0:T(8,128)} %param.16, bf16[768,1152]{1,0:T(8,128)(2,1)} %bitcast.69, bf16[768,1536]{1,0:T(8,128)(2,1)} %copy-done.4), kind=kOutput, calls=%fused_computation.28 | convolution fusion | flops 2739142656 | bytes 21823488 | tf_op jit(solution)/shard_map/dot_general | solution.py:116
  141.9 6.7 %all-to-all-start.2 = ((bf16[16,24,1152]{2,1,0:T(8,128)(2,1)}), bf16[16,24,1152]{2,1,0:T(8,128)(2,1)}, u32[]{:S(2)}, u32[]{:S(2)}) async-start(bf16[16,24,1152]{2,1,0:T(8,128)(2,1)} %bitcast.63), calls=%async_computation.3 | async-start | bytes 1769472 | tf_op jit(solution)/shard_map/all_to_all | solution.py:105
  148.6 1.3 fusion.31
  150.6 1.2 pad_clamp_fusion
  151.8 149.8 %collective-permute-done = bf16[1,1152,1536]{2,1,0:T(8,128)(2,1)} collective-permute-done((bf16[1,1152,1536]{2,1,0:T(8,128)(2,1)}, bf16[1,1152,1536]{2,1,0:T(8,128)(2,1)}, u32[]{:S(2)}, u32[]{:S(2)}) %collective-permute-start) | collective-permute-done | bytes 3538976 | tf_op jit(solution)/shard_map/ppermute | solution.py:21
  301.6 4.2 %broadcast_select_fusion = bf16[1,1152,1536]{2,1,0:T(8,128)(2,1)} fusion(bf16[1,1152,1536]{2,1,0:T(8,128)(2,1)} %collective-permute-done, bf16[1,1152,1536]{2,1,0:T(8,128)(2,1)} %fusion.19, pred[]{:T(512)S(6)} %ne.20), kind=kLoop, calls=%fused_computation.27 | loop fusion | flops 1769472 | bytes 10616833 | tf_op jit(solution)/shard_map/jit(_where)/select_n | solution.py:128
  305.8 9.9 %all-to-all-done.2 = bf16[16,24,1152]{2,1,0:T(8,128)(2,1)} async-done(((bf16[16,24,1152]{2,1,0:T(8,128)(2,1)}), bf16[16,24,1152]{2,1,0:T(8,128)(2,1)}, u32[]{:S(2)}, u32[]{:S(2)}) %all-to-all-start.2) | async-done | bytes 884768 | tf_op jit(solution)/shard_map/all_to_all | solution.py:105
  315.7 3.9 %gather_fusion.2 = bf16[256,1152]{1,0:T(8,128)(2,1)} fusion(bf16[384,1152]{1,0:T(8,128)(2,1)} %bitcast.11, s32[1024]{0:T(1024)} %pad_clamp_fusion), kind=kCustom, calls=%fused_computation.2 | custom fusion | bytes 1180672 | tf_op jit(solution)/shard_map/jit(_take)/gather | solution.py:112
  319.6 2.6 gather.23
  322.2 3.2 fusion.23
  (33 shorter events, 9.3 us)
Async XLA Ops:
  7.2 92.4 %copy-start = (bf16[1,1152,1536]{2,1,0:T(8,128)(2,1)S(1)}, bf16[1,1152,1536]{2,1,0:T(8,128)(2,1)}, u32[]{:S(2)}) copy-start(bf16[1,1152,1536]{2,1,0:T(8,128)(2,1)} %param.14) | copy-start | bytes 10616836
  7.2 92.4 %all-gather.5.cloned.1.call-start = ((), (), s32[]{:S(2)}) async-start(), calls=%async_computation.5 | async-start | bytes 2654208 | tf_op jit(solution)/shard_map/all_gather | solution.py:85
  10.6 0.6 copy-start.1
  17.1 4.8 %copy-start.3 = (s32[256,1]{0,1:T(1,128)}, s32[256,1]{0,1:T(1,128)S(1)}, u32[]{:S(2)}) copy-start(s32[256,1]{0,1:T(1,128)S(1)} %compare_select_fusion.1) | copy-start | bytes 3076
  36.8 7.0 %copy-start.2 = (pred[16,24]{1,0:T(8,128)(4,1)S(1)}, pred[16,24]{1,0:T(8,128)(4,1)}, u32[]{:S(2)}) copy-start(pred[16,24]{1,0:T(8,128)(4,1)} %broadcast_in_dim.72) | copy-start | bytes 1156
  73.9 37.5 %all-gather.3.cloned.1.call-start = ((), (), s32[]{:S(2)}) async-start(), calls=%async_computation.4 | async-start | bytes 2654208 | tf_op jit(solution)/shard_map/all_gather | solution.py:86
  99.3 42.6 %reduce-scatter.2.cloned.1.call-start = ((), (), s32[]{:S(2)}) async-start(), calls=%async_computation.6 | async-start | bytes 2654208 | tf_op jit(solution)/shard_map/reduce_scatter | solution.py:97
  119.4 1.4 copy-start.4
  140.3 161.3 %collective-permute-start = (bf16[1,1152,1536]{2,1,0:T(8,128)(2,1)}, bf16[1,1152,1536]{2,1,0:T(8,128)(2,1)}, u32[]{:S(2)}, u32[]{:S(2)}) collective-permute-start(bf16[1,1152,1536]{2,1,0:T(8,128)(2,1)} %fusion.19), channel_id=1, source_target_pairs={{0,8},{8,0},{1,9},{9,1},{2,10},{10,2},{3,11},{11,3},{4,12},{12,4},... | collective-permute-start | bytes 10616840 | tf_op jit(solution)/shard_map/ppermute | solution.py:21
  141.9 173.7 %all-to-all-start.2 = ((bf16[16,24,1152]{2,1,0:T(8,128)(2,1)}), bf16[16,24,1152]{2,1,0:T(8,128)(2,1)}, u32[]{:S(2)}, u32[]{:S(2)}) async-start(bf16[16,24,1152]{2,1,0:T(8,128)(2,1)} %bitcast.63), calls=%async_computation.3 | async-start | bytes 1769472 | tf_op jit(solution)/shard_map/all_to_all | solution.py:105
Sparse Core Ops, SparseCore 0:
  74.1 11.0 all-gather.4
  99.5 11.9 all-gather.2
  125.3 10.4 reduce-scatter.1
where the time goes:
time: 333 us; the launch traced here: 332 us
  waiting for transfers between devices  165 us (50%)
  blocking collectives  52.8 us (16%)
  local copies, waits for them, and re-layouts  35.9 us (11%)
  matrix products  33.7 us (10%)
  other arithmetic  22.7 us (7%)
  between operations  14.5 us (4%)
  starting transfers between devices  7.01 us (2%)
    ppermute x1, waiting for transfers between devices, partner(): return lax.ppermute(block, axis, route)  150 us
    all_to_all x1, blocking collectives, shards(): lax.all_to_all(x_buf, 'expert', split_axis=0, concat_axis=0, tiled=True)  27.4 us
    all_to_all x1, blocking collectives, shards(): lax.all_to_all(g_buf, 'expert', split_axis=0, concat_axis=0, tiled=True)  25.3 us
    dot_general x1, matrix products, shards(): lax.dot_general(x_rows, pre_grad, (((0,), (0,)), ((), ())), preferred_ele...  15.1 us
    all_to_all x1, waiting for transfers between devices, shards(): lax.all_to_all(own_rows.reshape(expert_count, capacity, model_width), 'ex...  9.91 us
    dot_general x1, matrix products, shards(): lax.dot_general(g_rows, w_out_local, (((1,), (1,)), ((), ())), preferred_...  7.95 us
    mul x3, local copies, waits for them, and re-layouts, shards(): gates[:, :, None] * out_grad[:, None, :].astype(jnp.float32)  6.8 us
    all_to_all x1, starting transfers between devices, shards(): lax.all_to_all(own_rows.reshape(expert_count, capacity, model_width), 'ex...  6.7 us
  transfers between devices with their start and end apart: 5, of which 3 were waited for; matrix products, arithmetic and copies ran while one was open for 9% of the time, Pallas kernels for 0%

commit v1 on v0

--- a/solution.py
+++ b/solution.py
@@ -9,6 +9,29 @@
 beta_one = 0.9
 beta_two = 0.999
 adam_eps = 1e-08
+
+
+def in_blocks(x, dim, devices):
+    dims = x.shape
+    pieces = x.reshape(*dims[:dim], devices, dims[dim] // devices, *dims[dim + 1 :])
+    return jnp.moveaxis(pieces, dim, 0)
+
+
+def joined_along(blocks, dim):
+    lengths = list(blocks.shape[1:])
+    lengths[dim] *= blocks.shape[0]
+    return jnp.moveaxis(blocks, 0, dim).reshape(lengths)
+
+
+def swapped_with_each(array, axis, split_dim, concat_dim):
+    size, mine = (lax.axis_size(axis), lax.axis_index(axis))
+    blocks = in_blocks(array, split_dim, size)
+    finished = [blocks[mine]]
+    for lap in range(1, size):
+        sent = blocks[mine ^ lap]
+        finished.append(lax.ppermute(sent, axis, [(i, i ^ lap) for i in range(size)]))
+    blocks = jnp.stack(finished)[mine ^ jnp.arange(size)]
+    return joined_along(blocks, concat_dim)
 
 
 def partner(block, axis, apart):
@@ -79,7 +102,7 @@
     x_buf, g_buf, where_to = pack_rows(expert_ids, tokens, grad_pair, lane_ids, capacity)
     x_recv, g_recv = (
         lax.all_to_all(x_buf, "expert", split_axis=0, concat_axis=0, tiled=True),
-        lax.all_to_all(g_buf, "expert", split_axis=0, concat_axis=0, tiled=True),
+        swapped_with_each(g_buf, "expert", 0, 0),
     )
     x_all, g_all = (
         lax.all_gather(x_recv, "dp", axis=0, tiled=True),

time: 333 us -> 344 us (1.033)
  blocking collectives: 52.8 us -> 0 us
  starting transfers between devices: 7.01 us -> 29.6 us
  waiting for transfers between devices: 165 us -> 185 us
  local copies, waits for them, and re-layouts: 35.9 us -> 55 us
    all_to_all x2 -> x0, blocking collectives: 52.8 us -> none  [the longest x1 27.4 us: shards(): lax.all_to_all(x_buf, 'expert', split_axis=0, concat_axis=0, tiled=True)]
    ppermute x0 -> x15, starting transfers between devices: none -> 17 us  [swapped_with_each(): lax.ppermute(sent, axis, [(i, i ^ lap) for i in range(size)])]
    unnamed x12 -> x24, local copies, waits for them, and re-layouts: 5.13 us -> 20.3 us
    ppermute x0 -> x15, waiting for transfers between devices: none -> 12.7 us  [swapped_with_each(): lax.ppermute(sent, axis, [(i, i ^ lap) for i in range(size)])]
    all_gather x1, waiting for transfers between devices: 0.02 us -> 5.83 us  [shards(): lax.all_gather(x_recv, 'dp', axis=0, tiled=True)]
    all_to_all x0 -> x1, starting transfers between devices: none -> 5.62 us  [shards(): lax.all_to_all(x_buf, 'expert', split_axis=0, concat_axis=0, tiled=True)]
  transfers between devices with their start and end apart: 5 -> 21, of which waited for: 3 -> 11; matrix products, arithmetic and copies ran while one was open for 9% -> 17% of each run, Pallas kernels for 0% -> 0%
where the time goes in v1:
time: 344 us; the launch traced here: 342 us
  waiting for transfers between devices  185 us (54%)
  local copies, waits for them, and re-layouts  55 us (16%)
  matrix products  33.8 us (10%)
  starting transfers between devices  29.6 us (9%)
  other arithmetic  23.7 us (7%)
  between operations  14.6 us (4%)
    ppermute x1, waiting for transfers between devices, partner(): return lax.ppermute(block, axis, route)  150 us
    unnamed x24, local copies, waits for them, and re-layouts  20.3 us
    ppermute x15, starting transfers between devices, swapped_with_each(): lax.ppermute(sent, axis, [(i, i ^ lap) for i in range(size)])  17 us
    dot_general x1, matrix products, shards(): lax.dot_general(x_rows, pre_grad, (((0,), (0,)), ((), ())), preferred_ele...  15.1 us
    ppermute x15, waiting for transfers between devices, swapped_with_each(): lax.ppermute(sent, axis, [(i, i ^ lap) for i in range(size)])  12.7 us
    all_to_all x1, waiting for transfers between devices, shards(): lax.all_to_all(own_rows.reshape(expert_count, capacity, model_width), 'ex...  9.92 us
    dot_general x1, matrix products, shards(): lax.dot_general(g_rows, w_out_local, (((1,), (1,)), ((), ())), preferred_...  7.95 us
    all_gather x1, waiting for transfers between devices, shards(): lax.all_gather(g_recv, 'dp', axis=0, tiled=True)  7 us
  transfers between devices with their start and end apart: 21, of which 11 were waited for; matrix products, arithmetic and copies ran while one was open for 17% of the time, Pallas kernels for 0%

profile of v1, /device:TPU:17, one launch (start us, length us, event | category | flops | bytes accessed | tf_op | source)
XLA Modules:
  0.0 342.1 jit_solution(1412385676071341798)
XLA Ops:
  7.8 1.7 copy.14
  17.1 1.6 scatter_custom_fusion
  19.9 2.3 mul.129
  22.1 3.0 mul.130
  26.6 1.5 mul.127
  30.2 2.2 multiply_convert_fusion
  32.5 4.7 %gather_fusion = bf16[384,1152]{1,0:T(8,128)(2,1)} fusion(bf16[256,1152]{1,0:T(8,128)(2,1)} %multiply_convert_fusion, s32[1024]{0:T(1024)S(1)} %get-tuple-element.23), kind=kCustom, calls=%fused_computation | custom fusion | bytes 1771008 | tf_op jit(solution)/shard_map/jit(_take)/gather | solution.py:79
  45.4 4.6 %gather_fusion.2 = bf16[384,1152]{1,0:T(8,128)(2,1)} fusion(bf16[128,1152]{1,0:T(8,128)(2,1)} %param.9, s32[1024]{0:T(1024)S(1)} %get-tuple-element.22), kind=kCustom, calls=%fused_computation.2 | custom fusion | bytes 1771008 | tf_op jit(solution)/shard_map/jit(_take)/gather | solution.py:75
  50.0 2.3 select_select_fusion
  52.3 5.6 %all-to-all-start = ((bf16[16,24,1152]{2,1,0:T(8,128)(2,1)}), bf16[16,24,1152]{2,1,0:T(8,128)(2,1)}, u32[]{:S(2)}, u32[]{:S(2)}) async-start(bf16[16,24,1152]{2,1,0:T(8,128)(2,1)} %select_select_fusion), calls=%async_computation | async-start | bytes 1769472 | tf_op jit(solution)/shard_map/all_to_all | solution.py:104
  58.0 2.1 collective-permute-start.5
  64.5 1.4 bitcast_dynamic-update-slice_fusion.12
  65.9 2.1 collective-permute-start.8
  72.1 2.3 collective-permute-done.5
  77.1 5.6 %collective-permute-done.7 = bf16[1,24,1152]{2,1,0:T(8,128)(2,1)S(1)} collective-permute-done((bf16[1,24,1152]{2,1,0:T(8,128)(2,1)}, bf16[1,24,1152]{2,1,0:T(8,128)(2,1)S(1)}, u32[]{:S(2)}, u32[]{:S(2)}) %collective-permute-start.7) | collective-permute-done | bytes 55328 | tf_op jit(solution)/shard_map/ppermute | solution.py:32
  84.4 2.7 collective-permute-start.13
  93.1 1.9 collective-permute-done.13
  96.4 1.5 collective-permute-done.14
  99.4 2.7 gather_fusion.1
  102.4 5.8 %all-gather.4.cloned.1.call-done = bf16[32,24,1152]{2,1,0:T(8,128)(2,1)} async-done(((bf16[16,24,1152]{2,1,0:T(8,128)(2,1)}), bf16[32,24,1152]{2,1,0:T(8,128)(2,1)}) %all-gather.4.cloned.1.call-update) | async-done | bytes 1769488 | tf_op jit(solution)/shard_map/all_gather | solution.py:108
  108.2 6.4 %fusion.16 = f32[768,1536]{1,0:T(8,128)} fusion(bf16[768,1152]{1,0:T(8,128)(2,1)} %bitcast.132, bf16[1,1152,1536]{2,1,0:T(8,128)(2,1)S(1)} %copy-done), kind=kOutput, calls=%fused_computation.25 | convolution fusion | flops 2717908992 | bytes 10027008 | tf_op jit(solution)/shard_map/dot_general | solution.py:115
  114.6 7.0 %all-gather.6.cloned.1.call-done = bf16[32,24,1152]{2,1,0:T(8,128)(2,1)} async-done(((bf16[16,24,1152]{2,1,0:T(8,128)(2,1)}), bf16[32,24,1152]{2,1,0:T(8,128)(2,1)}) %all-gather.6.cloned.1.call-update) | async-done | bytes 1769488 | tf_op jit(solution)/shard_map/all_gather | solution.py:109
  121.6 7.9 %fusion.13 = bf16[768,1536]{1,0:T(8,128)(2,1)S(1)} fusion(f32[768,1536]{1,0:T(8,128)} %fusion.16, bf16[768,1152]{1,0:T(8,128)(2,1)} %bitcast.134, bf16[1,1536,1152]{2,1,0:T(8,128)(2,1)} %param.15), kind=kOutput, calls=%fused_computation.22 | convolution fusion | flops 2740322304 | bytes 12386304 | tf_op jit(solution)/shard_map/dot_general | solution.py:116
  131.0 4.4 %fusion.20 = bf16[768,1152]{1,0:T(8,128)(2,1)} fusion(bf16[768,1536]{1,0:T(8,128)(2,1)S(1)} %fusion.13, bf16[1,1152,1536]{2,1,0:T(8,128)(2,1)S(1)} %copy-done), kind=kOutput, calls=%fused_computation.30 | convolution fusion | flops 2718793728 | bytes 7667712 | tf_op jit(solution)/shard_map/dot_general | solution.py:121
  135.4 15.1 %fusion.19 = bf16[1,1152,1536]{2,1,0:T(8,128)(2,1)} fusion(f32[1,1152,1536]{2,1,0:T(8,128)} %param.17, f32[1,1152,1536]{2,1,0:T(8,128)} %param.16, bf16[768,1152]{1,0:T(8,128)(2,1)} %bitcast.133, bf16[768,1536]{1,0:T(8,128)(2,1)} %copy-done.3), kind=kOutput, calls=%fused_computation.29 | convolution fusion | flops 2739142656 | bytes 21823488 | tf_op jit(solution)/shard_map/dot_general | solution.py:139
  152.1 6.7 %all-to-all-start.1 = ((bf16[16,24,1152]{2,1,0:T(8,128)(2,1)}), bf16[16,24,1152]{2,1,0:T(8,128)(2,1)}, u32[]{:S(2)}, u32[]{:S(2)}) async-start(bf16[16,24,1152]{2,1,0:T(8,128)(2,1)} %bitcast.127), calls=%async_computation.2 | async-start | bytes 1769472 | tf_op jit(solution)/shard_map/all_to_all | solution.py:128
  162.0 149.8 %collective-permute-done.15 = bf16[1,1152,1536]{2,1,0:T(8,128)(2,1)} collective-permute-done((bf16[1,1152,1536]{2,1,0:T(8,128)(2,1)}, bf16[1,1152,1536]{2,1,0:T(8,128)(2,1)}, u32[]{:S(2)}, u32[]{:S(2)}) %collective-permute-start.15) | collective-permute-done | bytes 3538976 | tf_op jit(solution)/shard_map/ppermute | solution.py:44
  311.8 4.2 %broadcast_select_fusion = bf16[1,1152,1536]{2,1,0:T(8,128)(2,1)} fusion(bf16[1,1152,1536]{2,1,0:T(8,128)(2,1)} %collective-permute-done.15, bf16[1,1152,1536]{2,1,0:T(8,128)(2,1)} %fusion.19, pred[]{:T(512)S(6)} %ne.20), kind=kLoop, calls=%fused_computation.28 | loop fusion | flops 1769472 | bytes 10616833 | tf_op jit(solution)/shard_map/jit(_where)/select_n | solution.py:151
  316.0 9.9 %all-to-all-done.1 = bf16[16,24,1152]{2,1,0:T(8,128)(2,1)} async-done(((bf16[16,24,1152]{2,1,0:T(8,128)(2,1)}), bf16[16,24,1152]{2,1,0:T(8,128)(2,1)}, u32[]{:S(2)}, u32[]{:S(2)}) %all-to-all-start.1) | async-done | bytes 884768 | tf_op jit(solution)/shard_map/all_to_all | solution.py:128
  325.9 3.9 %gather_fusion.3 = bf16[256,1152]{1,0:T(8,128)(2,1)} fusion(bf16[384,1152]{1,0:T(8,128)(2,1)} %bitcast.43, s32[1024]{0:T(1024)} %pad_clamp_fusion), kind=kCustom, calls=%fused_computation.3 | custom fusion | bytes 1180672 | tf_op jit(solution)/shard_map/jit(_take)/gather | solution.py:135
  329.8 2.6 gather.27
  332.4 3.2 fusion.23
  (80 shorter events, 48.5 us)
Async XLA Ops:
  7.2 101.1 %copy-start = (bf16[1,1152,1536]{2,1,0:T(8,128)(2,1)S(1)}, bf16[1,1152,1536]{2,1,0:T(8,128)(2,1)}, u32[]{:S(2)}) copy-start(bf16[1,1152,1536]{2,1,0:T(8,128)(2,1)} %param.14) | copy-start | bytes 10616836
  10.5 0.6 copy-start.1
  17.1 12.4 %copy-start.2 = (s32[256,1]{0,1:T(1,128)}, s32[256,1]{0,1:T(1,128)S(1)}, u32[]{:S(2)}) copy-start(s32[256,1]{0,1:T(1,128)S(1)} %compare_select_fusion.1) | copy-start | bytes 3076
  39.6 18.4 %collective-permute-start = (bf16[1,24,1152]{2,1,0:T(8,128)(2,1)}, bf16[1,24,1152]{2,1,0:T(8,128)(2,1)}, u32[]{:S(2)}, u32[]{:S(2)}) collective-permute-start(bf16[1,24,1152]{2,1,0:T(8,128)(2,1)} %get-tuple-element.18), channel_id=1, source_target_pairs={{0,1},{1,0},{2,3},{3,2},{4,5},{5,4},{6,7},{7,6},{8,9},{9,8},{10,11... | collective-permute-start | bytes 165896 | tf_op jit(solution)/shard_map/ppermute | solution.py:32
  40.8 20.7 %collective-permute-start.1 = (bf16[1,24,1152]{2,1,0:T(8,128)(2,1)}, bf16[1,24,1152]{2,1,0:T(8,128)(2,1)}, u32[]{:S(2)}, u32[]{:S(2)}) collective-permute-start(bf16[1,24,1152]{2,1,0:T(8,128)(2,1)} %get-tuple-element.17), channel_id=1, source_target_pairs={{0,2},{1,3},{2,0},{3,1},{4,6},{5,7},{6,4},{7,5},{8,10},{9,11},{10,... | collective-permute-start | bytes 165896 | tf_op jit(solution)/shard_map/ppermute | solution.py:32
  42.1 22.1 %collective-permute-start.2 = (bf16[1,24,1152]{2,1,0:T(8,128)(2,1)}, bf16[1,24,1152]{2,1,0:T(8,128)(2,1)}, u32[]{:S(2)}, u32[]{:S(2)}) collective-permute-start(bf16[1,24,1152]{2,1,0:T(8,128)(2,1)} %get-tuple-element.16), channel_id=1, source_target_pairs={{0,3},{1,2},{2,1},{3,0},{4,7},{5,6},{6,5},{7,4},{8,11},{9,10},{10,... | collective-permute-start | bytes 165896 | tf_op jit(solution)/shard_map/ppermute | solution.py:32
  42.3 23.6 %collective-permute-start.3 = (bf16[1,24,1152]{2,1,0:T(8,128)(2,1)}, bf16[1,24,1152]{2,1,0:T(8,128)(2,1)}, u32[]{:S(2)}, u32[]{:S(2)}) collective-permute-start(bf16[1,24,1152]{2,1,0:T(8,128)(2,1)} %get-tuple-element.15), channel_id=1, source_target_pairs={{0,4},{1,5},{2,6},{3,7},{4,0},{5,1},{6,2},{7,3},{8,12},{9,13},{10,... | collective-permute-start | bytes 165896 | tf_op jit(solution)/shard_map/ppermute | solution.py:32
  43.6 25.9 %collective-permute-start.4 = (bf16[1,24,1152]{2,1,0:T(8,128)(2,1)}, bf16[1,24,1152]{2,1,0:T(8,128)(2,1)}, u32[]{:S(2)}, u32[]{:S(2)}) collective-permute-start(bf16[1,24,1152]{2,1,0:T(8,128)(2,1)} %get-tuple-element.14), channel_id=1, source_target_pairs={{0,5},{1,4},{2,7},{3,6},{4,1},{5,0},{6,3},{7,2},{8,13},{9,12},{10,... | collective-permute-start | bytes 165896 | tf_op jit(solution)/shard_map/ppermute | solution.py:32
  52.3 37.6 %all-to-all-start = ((bf16[16,24,1152]{2,1,0:T(8,128)(2,1)}), bf16[16,24,1152]{2,1,0:T(8,128)(2,1)}, u32[]{:S(2)}, u32[]{:S(2)}) async-start(bf16[16,24,1152]{2,1,0:T(8,128)(2,1)} %select_select_fusion), calls=%async_computation | async-start | bytes 1769472 | tf_op jit(solution)/shard_map/all_to_all | solution.py:104
  57.9 50.3 %all-gather.4.cloned.1.call-start = ((), (), s32[]{:S(2)}) async-start(), calls=%async_computation.3 | async-start | bytes 2654208 | tf_op jit(solution)/shard_map/all_gather | solution.py:108
  58.0 16.4 %collective-permute-start.5 = (bf16[1,24,1152]{2,1,0:T(8,128)(2,1)}, bf16[1,24,1152]{2,1,0:T(8,128)(2,1)S(1)}, u32[]{:S(2)}, u32[]{:S(2)}) collective-permute-start(bf16[1,24,1152]{2,1,0:T(8,128)(2,1)} %get-tuple-element.13), channel_id=1, source_target_pairs={{0,6},{1,7},{2,4},{3,5},{4,2},{5,3},{6,0},{7,1},{8,14},{9,15},{10,... | collective-permute-start | bytes 165896 | tf_op jit(solution)/shard_map/ppermute | solution.py:32
  61.6 14.9 %collective-permute-start.6 = (bf16[1,24,1152]{2,1,0:T(8,128)(2,1)}, bf16[1,24,1152]{2,1,0:T(8,128)(2,1)S(1)}, u32[]{:S(2)}, u32[]{:S(2)}) collective-permute-start(bf16[1,24,1152]{2,1,0:T(8,128)(2,1)} %get-tuple-element.12), channel_id=1, source_target_pairs={{0,7},{1,6},{2,5},{3,4},{4,3},{5,2},{6,1},{7,0},{8,15},{9,14},{10,... | collective-permute-start | bytes 165896 | tf_op jit(solution)/shard_map/ppermute | solution.py:32
  64.2 18.5 %collective-permute-start.7 = (bf16[1,24,1152]{2,1,0:T(8,128)(2,1)}, bf16[1,24,1152]{2,1,0:T(8,128)(2,1)S(1)}, u32[]{:S(2)}, u32[]{:S(2)}) collective-permute-start(bf16[1,24,1152]{2,1,0:T(8,128)(2,1)} %get-tuple-element.11), channel_id=1, source_target_pairs={{0,8},{1,9},{2,10},{3,11},{4,12},{5,13},{6,14},{7,15},{8,0},{9,1},... | collective-permute-start | bytes 165896 | tf_op jit(solution)/shard_map/ppermute | solution.py:32
  65.9 18.5 %collective-permute-start.8 = (bf16[1,24,1152]{2,1,0:T(8,128)(2,1)}, bf16[1,24,1152]{2,1,0:T(8,128)(2,1)S(1)}, u32[]{:S(2)}, u32[]{:S(2)}) collective-permute-start(bf16[1,24,1152]{2,1,0:T(8,128)(2,1)} %get-tuple-element.10), channel_id=1, source_target_pairs={{0,9},{1,8},{2,11},{3,10},{4,13},{5,12},{6,15},{7,14},{8,1},{9,0},... | collective-permute-start | bytes 165896 | tf_op jit(solution)/shard_map/ppermute | solution.py:32
  69.4 18.3 %collective-permute-start.9 = (bf16[1,24,1152]{2,1,0:T(8,128)(2,1)}, bf16[1,24,1152]{2,1,0:T(8,128)(2,1)S(1)}, u32[]{:S(2)}, u32[]{:S(2)}) collective-permute-start(bf16[1,24,1152]{2,1,0:T(8,128)(2,1)} %get-tuple-element.9), channel_id=1, source_target_pairs={{0,10},{1,11},{2,8},{3,9},{4,14},{5,15},{6,12},{7,13},{8,2},{9,3},... | collective-permute-start | bytes 165896 | tf_op jit(solution)/shard_map/ppermute | solution.py:32
  74.4 14.8 %collective-permute-start.10 = (bf16[1,24,1152]{2,1,0:T(8,128)(2,1)}, bf16[1,24,1152]{2,1,0:T(8,128)(2,1)S(1)}, u32[]{:S(2)}, u32[]{:S(2)}) collective-permute-start(bf16[1,24,1152]{2,1,0:T(8,128)(2,1)} %get-tuple-element.8), channel_id=1, source_target_pairs={{0,11},{1,10},{2,9},{3,8},{4,15},{5,14},{6,13},{7,12},{8,3},{9,2},... | collective-permute-start | bytes 165896 | tf_op jit(solution)/shard_map/ppermute | solution.py:32
  76.5 13.5 %collective-permute-start.11 = (bf16[1,24,1152]{2,1,0:T(8,128)(2,1)}, bf16[1,24,1152]{2,1,0:T(8,128)(2,1)}, u32[]{:S(2)}, u32[]{:S(2)}) collective-permute-start(bf16[1,24,1152]{2,1,0:T(8,128)(2,1)} %get-tuple-element.7), channel_id=1, source_target_pairs={{0,12},{1,13},{2,14},{3,15},{4,8},{5,9},{6,10},{7,11},{8,4},{9,5},... | collective-permute-start | bytes 165896 | tf_op jit(solution)/shard_map/ppermute | solution.py:32
  82.7 9.0 %collective-permute-start.12 = (bf16[1,24,1152]{2,1,0:T(8,128)(2,1)}, bf16[1,24,1152]{2,1,0:T(8,128)(2,1)}, u32[]{:S(2)}, u32[]{:S(2)}) collective-permute-start(bf16[1,24,1152]{2,1,0:T(8,128)(2,1)} %get-tuple-element.6), channel_id=1, source_target_pairs={{0,13},{1,12},{2,15},{3,14},{4,9},{5,8},{6,11},{7,10},{8,5},{9,4},... | collective-permute-start | bytes 165896 | tf_op jit(solution)/shard_map/ppermute | solution.py:32
  84.4 10.6 %collective-permute-start.13 = (bf16[1,24,1152]{2,1,0:T(8,128)(2,1)}, bf16[1,24,1152]{2,1,0:T(8,128)(2,1)}, u32[]{:S(2)}, u32[]{:S(2)}) collective-permute-start(bf16[1,24,1152]{2,1,0:T(8,128)(2,1)} %get-tuple-element.5), channel_id=1, source_target_pairs={{0,14},{1,15},{2,12},{3,13},{4,10},{5,11},{6,8},{7,9},{8,6},{9,7},... | collective-permute-start | bytes 165896 | tf_op jit(solution)/shard_map/ppermute | solution.py:32
  87.8 10.2 %collective-permute-start.14 = (bf16[1,24,1152]{2,1,0:T(8,128)(2,1)}, bf16[1,24,1152]{2,1,0:T(8,128)(2,1)}, u32[]{:S(2)}, u32[]{:S(2)}) collective-permute-start(bf16[1,24,1152]{2,1,0:T(8,128)(2,1)} %get-tuple-element.4), channel_id=1, source_target_pairs={{0,15},{1,14},{2,13},{3,12},{4,11},{5,10},{6,9},{7,8},{8,7},{9,6},... | collective-permute-start | bytes 165896 | tf_op jit(solution)/shard_map/ppermute | solution.py:32
  89.9 31.7 %all-gather.6.cloned.1.call-start = ((), (), s32[]{:S(2)}) async-start(), calls=%async_computation.5 | async-start | bytes 2654208 | tf_op jit(solution)/shard_map/all_gather | solution.py:109
  102.1 50.0 %reduce-scatter.2.cloned.1.call-start = ((), (), s32[]{:S(2)}) async-start(), calls=%async_computation.4 | async-start | bytes 2654208 | tf_op jit(solution)/shard_map/reduce_scatter | solution.py:120
  129.6 1.4 copy-start.3
  150.5 161.3 %collective-permute-start.15 = (bf16[1,1152,1536]{2,1,0:T(8,128)(2,1)}, bf16[1,1152,1536]{2,1,0:T(8,128)(2,1)}, u32[]{:S(2)}, u32[]{:S(2)}) collective-permute-start(bf16[1,1152,1536]{2,1,0:T(8,128)(2,1)} %fusion.19), channel_id=1, source_target_pairs={{0,8},{8,0},{1,9},{9,1},{2,10},{10,2},{3,11},{11,3},{4,12},{12,4},... | collective-permute-start | bytes 10616840 | tf_op jit(solution)/shard_map/ppermute | solution.py:44
  152.1 173.8 %all-to-all-start.1 = ((bf16[16,24,1152]{2,1,0:T(8,128)(2,1)}), bf16[16,24,1152]{2,1,0:T(8,128)(2,1)}, u32[]{:S(2)}, u32[]{:S(2)}) async-start(bf16[16,24,1152]{2,1,0:T(8,128)(2,1)} %bitcast.127), calls=%async_computation.2 | async-start | bytes 1769472 | tf_op jit(solution)/shard_map/all_to_all | solution.py:128
Sparse Core Ops, SparseCore 0:
  90.0 18.1 all-gather.3
  110.3 11.2 all-gather.5
  135.5 10.4 reduce-scatter.1
